TPU v7x, 768 devices: a whole 4x8x12 slice. The times are simulated.
768 devices in a mesh: section: 24 (over z, x_hi), tensor: 32 (over y, x_lo, core).
Axes of the slice: x: 4 (x_hi: 2, x_lo: 2; x = x_hi * 2 + x_lo), y: 8, z: 12, core: 2. Of those that a mesh axis runs over, the one named last changes fastest.
Arguments:
- text: bfloat16 [24, 256, 8192], P('section', 'tensor'), may hold values from -6 to 6
- features: bfloat16 [192, 8192], P(None, 'tensor'), may hold values from -6 to 6
- in_gain: bfloat16 [24, 8192], P('section'), may hold values from 0.5 to 1.5
- w_query: bfloat16 [24, 8192, 4096], P('section', None, 'tensor'), may hold values from -0.0625 to 0.0625
- q_gain: bfloat16 [24, 128], P('section'), may hold values from 0.099609375 to 1.8984375
- w_key_value: bfloat16 [24, 8192, 2048], P('section', 'tensor'), may hold values from -0.0625 to 0.0625
- k_gain: bfloat16 [24, 128], P('section'), may hold values from 0.099609375 to 1.8984375
- tile_count: int32 [2], replicated, may hold values from 1 to 4, as said below
- image_start: int32 [2], replicated, may hold values from 1 to 127
- grad_out: bfloat16 [24, 256, 4096], P('section', None, 'tensor'), may hold values from -6 to 6
Outputs:
- attended: bfloat16 [24, 256, 4096], P('section', None, 'tensor')
- feature_grad: float32 [192, 8192], P('section', 'tensor')
Inputs may be any that keep to these rules, and one draw needn't show every extreme that they name: `tile_count`: some sample has 4 tiles.
All inputs are finite; a program needn't handle non-finite values.
Results may differ from a plain program's by a relative error of at most 0.0089.
Values may be sent and summed in bfloat16 or wider, within the bound.
A program may use at most 32 MiB of HBM per device.

v0:
```python
import jax
import jax.numpy as jnp
from jax import lax
from jax.sharding import PartitionSpec as P

KV_HEADS = 8
HEAD_DIM = 128
TILES = 4
TILE_LEN = 24
TXT_TOK = 128
MB = 2


eps = 1e-05


def rms_scale(values, norm_gain):
    inverse = lax.rsqrt(jnp.mean(values * values, axis=-1, keepdims=True) + eps)
    return values * inverse * norm_gain


def shards(
    text, features, in_gain, w_query, q_gain, w_key_value, k_gain, tile_count, image_start, grad_out
):
    score_scale = HEAD_DIM ** (-0.5)
    heads_local = w_query.shape[2] // HEAD_DIM
    image_slots = TILES * TILE_LEN
    total_rows = features.shape[0]
    tensor_count = lax.axis_size("tensor")
    per_kv = tensor_count // KV_HEADS
    kv_head = lax.axis_index("tensor") // per_kv
    layer_gain = in_gain[0].astype(jnp.float32)
    query_gain = q_gain[0].astype(jnp.float32)
    key_gain = k_gain[0].astype(jnp.float32)
    weight_q = w_query[0]
    weight_kv = w_key_value[0]
    piece = lax.all_gather(text[0], "tensor", axis=0, tiled=True)
    normed = rms_scale(piece.astype(jnp.float32), layer_gain).astype(jnp.bfloat16)
    raw_q = jnp.dot(normed, weight_q, preferred_element_type=jnp.float32)
    raw_q = raw_q.reshape(piece.shape[0], heads_local, HEAD_DIM)
    queries_all = (
        rms_scale(raw_q, query_gain)
        .astype(jnp.bfloat16)
        .reshape(piece.shape[0], heads_local * HEAD_DIM)
    )
    partial_value = jnp.dot(features, weight_kv, preferred_element_type=jnp.float32)
    kv_full = lax.psum(partial_value, "tensor")
    key_flat = lax.dynamic_slice_in_dim(kv_full, kv_head * HEAD_DIM, HEAD_DIM, 1)
    value_flat = lax.dynamic_slice_in_dim(
        kv_full, KV_HEADS * HEAD_DIM + kv_head * HEAD_DIM, HEAD_DIM, 1
    )
    key_raw = key_flat.reshape(MB, image_slots, HEAD_DIM)
    values = value_flat.astype(jnp.bfloat16).reshape(MB, image_slots, HEAD_DIM)
    inverse = lax.rsqrt(jnp.mean(key_raw * key_raw, axis=-1, keepdims=True) + eps)
    key_hat = key_raw * inverse
    normed_keys = (key_hat * key_gain).astype(jnp.bfloat16)
    key_live = jnp.arange(image_slots, dtype=jnp.int32)[None, :] < (tile_count * TILE_LEN)[:, None]
    row_live = (jnp.arange(TXT_TOK, dtype=jnp.int32)[None, :] >= image_start[:, None]).astype(
        jnp.float32
    )
    row_mask = row_live[:, :, None, None]
    queries = queries_all.reshape(MB, TXT_TOK, heads_local, HEAD_DIM)
    scores = (
        jnp.einsum("bthd,bjd->bhtj", queries, normed_keys, preferred_element_type=jnp.float32)
        * score_scale
    )
    exponent = jnp.where(key_live[:, None, None, :], jnp.exp(scores), 0.0)
    probs = exponent / jnp.sum(exponent, axis=-1, keepdims=True)
    weights = probs.astype(jnp.bfloat16)
    head_out = (
        jnp.einsum("bhtj,bjd->bthd", weights, values, preferred_element_type=jnp.float32) * row_mask
    )
    attended = head_out.reshape(1, MB * TXT_TOK, heads_local * HEAD_DIM).astype(jnp.bfloat16)
    upstream = (
        grad_out[0].reshape(MB, TXT_TOK, heads_local, HEAD_DIM).astype(jnp.float32) * row_mask
    ).astype(jnp.bfloat16)
    d_weights = jnp.einsum("bthd,bjd->bhtj", upstream, values, preferred_element_type=jnp.float32)
    d_scores = (
        probs * (d_weights - jnp.sum(probs * d_weights, axis=-1, keepdims=True)) * score_scale
    ).astype(jnp.bfloat16)
    d_keys = jnp.einsum("bhtj,bthd->bjd", d_scores, queries, preferred_element_type=jnp.float32)
    d_values = jnp.einsum("bhtj,bthd->bjd", weights, upstream, preferred_element_type=jnp.float32)
    scaled = d_keys * key_gain
    d_raw = inverse * (scaled - key_hat * jnp.mean(key_hat * scaled, axis=-1, keepdims=True))
    own_piece = jnp.concatenate(
        [d_raw.astype(jnp.bfloat16), d_values.astype(jnp.bfloat16)], axis=-1
    )
    own_piece = own_piece.reshape(total_rows, 2 * HEAD_DIM)
    gathered = lax.all_gather(own_piece, "tensor", axis=0, tiled=True)
    grouped = (
        gathered.reshape(KV_HEADS, per_kv, total_rows, 2, HEAD_DIM).astype(jnp.float32).sum(axis=1)
    )
    d_kv = (
        jnp.transpose(grouped, (1, 2, 0, 3))
        .reshape(total_rows, 2 * KV_HEADS * HEAD_DIM)
        .astype(jnp.bfloat16)
    )
    feature_grad = lax.psum_scatter(
        lax.dot_general(
            d_kv, weight_kv, (((1,), (1,)), ((), ())), preferred_element_type=jnp.float32
        ),
        "section",
        scatter_dimension=0,
        tiled=True,
    )
    return (attended, feature_grad)


def solution(mesh):
    return jax.shard_map(
        shards,
        mesh=mesh,
        in_specs=(
            P("section", "tensor", None),
            P(None, "tensor"),
            P("section", None),
            P("section", None, "tensor"),
            P("section", None),
            P("section", "tensor", None),
            P("section", None),
            P(),
            P(),
            P("section", None, "tensor"),
        ),
        out_specs=(P("section", None, "tensor"), P("section", "tensor")),
        check_vma=False,
    )
```

profile of v0, /device:TPU:1, one launch (start us, length us, event | category | flops | bytes accessed | tf_op | source)
XLA Modules:
  0.0 800.7 jit_solution(12485249614634750785)
XLA Ops:
  7.3 3.0 fusion.17
  10.3 0.7 all-gather.6.cloned.1.call-update
  11.4 248.4 %all-reduce.2.cloned.1.call-done = f32[192,2048]{1,0:T(8,128)} async-done(((f32[192,2048]{1,0:T(8,128)}), f32[192,2048]{1,0:T(8,128)}) %all-reduce.2.cloned.1.call-update) | async-done | bytes 1572880 | tf_op jit(solution)/shard_map/psum | solution.py:47
  259.7 1.0 multiply_reduce_fusion.3
  260.7 0.1 rsqrt.28
  260.8 0.9 dynamic-slice_convert_fusion
  261.7 73.8 %all-gather.6.cloned.1.call-done = bf16[1,256,8192]{2,1,0:T(8,128)(2,1)} async-done(((bf16[1,8,8192]{2,1,0:T(8,128)(2,1)}), bf16[1,256,8192]{2,1,0:T(8,128)(2,1)}) %all-gather.6.cloned.1.call-update) | async-done | bytes 4194320 | tf_op jit(solution)/shard_map/all_gather | solution.py:37
  335.5 3.3 fusion
  338.8 0.2 copy-done.1
  339.0 1.5 multiply_reduce_fusion
  340.5 0.1 multiply_convert_fusion
  340.7 0.2 fusion.35
  340.9 0.2 convolution_convert_fusion
  341.1 0.2 multiply_reduce_fusion.2
  341.4 0.2 multiply_reduce_fusion.1
  341.7 0.1 multiply_convert_fusion.1
  341.8 0.6 pad_maximum_fusion
  342.5 71.3 %all-gather.4.cloned.1.call-done = bf16[6144,256]{1,0:T(8,128)(2,1)} async-done(((bf16[192,256]{1,0:T(8,128)(2,1)}), bf16[6144,256]{1,0:T(8,128)(2,1)}) %all-gather.4.cloned.1.call-update) | async-done | bytes 3145744 | tf_op jit(solution)/shard_map/all_gather | solution.py:89
  413.8 5.5 convert_element_type.126
  419.3 6.4 reduce.5
  425.7 0.9 copy.12
  426.6 2.4 fusion.15
  429.1 0.9 fusion.12
  429.9 364.2 %reduce-scatter.2.cloned.1.call-done = f32[8,256]{1,0:T(8,128)} async-done(((f32[192,256]{1,0:T(8,128)}), f32[8,256]{1,0:T(8,128)}) %reduce-scatter.2.cloned.1.call-update) | async-done | bytes 8208 | tf_op jit(solution)/shard_map/reduce_scatter | solution.py:98
  (32 shorter events, 0.5 us)
Async XLA Ops:
  7.2 331.6 %copy-start = (bf16[1,8192,128]{2,1,0:T(8,128)(2,1)S(1)}, bf16[1,8192,128]{2,1,0:T(8,128)(2,1)}, u32[]{:S(2)}) copy-start(bf16[1,8192,128]{2,1,0:T(8,128)(2,1)} %param.13) | copy-start | bytes 6291460
  7.2 3.9 copy-start.2
  7.2 4.0 copy-start.4
  7.2 4.0 copy-start.5
  7.2 4.0 copy-start.6
  7.2 4.1 copy-start.7
  7.2 252.5 %all-reduce.2.cloned.1.call-start = ((), (), s32[]{:S(2)}) async-start(), calls=%async_computation.1 | async-start | bytes 3145728 | tf_op jit(solution)/shard_map/psum | solution.py:47
  10.3 325.3 %all-gather.6.cloned.1.call-start = ((), (), s32[]{:S(2)}) async-start(), calls=%async_computation.4 | async-start | bytes 4325376 | tf_op jit(solution)/shard_map/all_gather | solution.py:37
  11.0 402.8 %all-gather.4.cloned.1.call-start = ((), (), s32[]{:S(2)}) async-start(), calls=%async_computation.2 | async-start | bytes 3244032 | tf_op jit(solution)/shard_map/all_gather | solution.py:89
  335.5 3.4 copy-start.1
  339.0 1.9 copy-start.3
  342.5 451.7 %reduce-scatter.2.cloned.1.call-start = ((), (), s32[]{:S(2)}) async-start(), calls=%async_computation.3 | async-start | bytes 204800 | tf_op jit(solution)/shard_map/reduce_scatter | solution.py:98
Sparse Core Ops, SparseCore 0:
  11.2 248.4 all-reduce.1
  262.2 73.3 all-gather.5
  342.6 71.1 all-gather.3
  429.2 364.9 reduce-scatter.1
where the time goes:
time: 809 us; the launch traced here: 801 us
  waiting for transfers between devices  758 us (94%)
  between operations  14 us (2%)
  other arithmetic  11.7 us (1%)
  matrix products  8.75 us (1%)
    reduce_scatter x1, waiting for transfers between devices, shards(): lax.psum_scatter(lax.dot_general(d_kv, weight_kv, (((1,), (1,)), ((), ())...  364 us
    psum x1, waiting for transfers between devices, shards(): kv_full = lax.psum(partial_value, 'tensor')  248 us
    all_gather x1, waiting for transfers between devices, shards(): piece = lax.all_gather(text[0], 'tensor', axis=0, tiled=True)  73.8 us
    all_gather x1, waiting for transfers between devices, shards(): gathered = lax.all_gather(own_piece, 'tensor', axis=0, tiled=True)  71.3 us
  transfers between devices with their start and end apart: 4, of which 4 were waited for; matrix products, arithmetic and copies ran while one was open for 0% of the time, Pallas kernels for 0%

commit v1 on v0

v1 whole, which is shorter than its diff:
```python
import functools

import jax
import jax.numpy as jnp
from jax import lax
from jax.experimental import pallas as pl
from jax.experimental.pallas import tpu as pltpu
from jax.sharding import PartitionSpec as P

KV_HEADS = 8
HEAD_DIM = 128
TILES = 4
TILE_LEN = 24
TXT_TOK = 128
MB = 2
SLOTS = TILES * TILE_LEN
IMG = MB * SLOTS
EPS = 1e-05
Y = 8
LANES = 4
N_TENSOR = Y * LANES
N_SECTION = 24
D = 8192
COLS = 256
QUARTER = IMG // LANES
CHUNK = IMG // N_SECTION
SCALE = HEAD_DIM ** (-0.5)
MESH = pl.DeviceIdType.MESH
F32 = jnp.float32
BF16 = jnp.bfloat16

POSITIONS = [(0, 0), (0, 1)]
for _d in range(1, 5):
    POSITIONS.append((-_d, 0))
    if _d < 4:
        POSITIONS.append((_d, 0))
        POSITIONS.append((-_d, 1))
    POSITIONS.append((_d, 1))
POS = {p: i for i, p in enumerate(POSITIONS)}


def last_of(sign, other):
    return 4 if (sign < 0) == (other == 0) else 3


def dotf(a, b, dims):
    return lax.dot_general(a, b, (dims, ((), ())), preferred_element_type=F32)


def kernel(
    text_ref, feat_ref, ing_ref, wq_hbm, qg_ref, wkv_hbm, kg_ref, tc_ref, is_ref, go_ref,
    att_ref, fg_ref,
    wq, wkv, txt, raw_q, part, p_send, p_recv, csum, up_s, up_r, dn_s, dn_r,
    x_s, x_r, kv, dq_s, dq_r, gath, grad, sec_s, sec_r,
    w_sem, txt_send, txt_recv, gat_send, gat_recv, kv_send, kv_recv, q_send, q_recv, s_send, s_recv,
):
    sec = lax.axis_index("section")
    me = lax.axis_index("tensor")
    y = me // LANES
    lane = me % LANES
    xl = lane // 2
    core = lane % 2

    def tid(y_at, x_at, c_at):
        return y_at * LANES + x_at * 2 + c_at

    sib = tid(y, xl, 1 - core)
    xnb = tid(y, 1 - xl, core)
    diag = tid(y, 1 - xl, 1 - core)
    yup = tid((y + 1) % Y, xl, core)
    ydn = tid((y + Y - 1) % Y, xl, core)

    def dev(t):
        return {"tensor": t, "section": sec}

    started = []

    def send(src, dst, s_sem, r_sem, to):
        copy = pltpu.make_async_remote_copy(
            src_ref=src, dst_ref=dst, send_sem=s_sem, recv_sem=r_sem, device_id=to, device_id_type=MESH
        )
        copy.start()
        started.append(copy)

    def wait_recv(dst, s_sem, r_sem):
        pltpu.make_async_remote_copy(
            src_ref=dst, dst_ref=dst, send_sem=s_sem, recv_sem=r_sem, device_id=dev(sib), device_id_type=MESH
        ).wait_recv()

    barrier = pltpu.get_barrier_semaphore()
    for k in range(1, N_SECTION):
        pl.semaphore_signal(
            barrier, inc=1, device_id={"section": (sec + k) % N_SECTION, "tensor": me}, device_id_type=MESH
        )
    for t in (yup, ydn, xnb, sib, diag):
        pl.semaphore_signal(barrier, inc=1, device_id=dev(t), device_id_type=MESH)

    load_kv = pltpu.make_async_copy(wkv_hbm, wkv, w_sem.at[0])
    load_q = pltpu.make_async_copy(wq_hbm, wq, w_sem.at[1])
    load_kv.start()
    load_q.start()

    own = text_ref[...].astype(F32)
    inv = lax.rsqrt(jnp.mean(own * own, axis=-1, keepdims=True) + EPS)
    txt[me] = (own * inv * ing_ref[...].astype(F32)).astype(BF16)

    load_kv.wait()
    part[...] = jnp.dot(feat_ref[...], wkv[...], preferred_element_type=F32)
    p_send[...] = part[pl.ds(pl.multiple_of((1 - core) * SLOTS, SLOTS), SLOTS), :].astype(BF16)

    pl.semaphore_wait(barrier, N_SECTION - 1 + 5)

    def block(y_at, other, c_at):
        return tid(y_at, xl + other - 2 * xl * other, c_at)

    def at_pos(p, c_at):
        return block((y + p[0] + Y) % Y, p[1], c_at)

    class Gather:
        def __init__(self, buf, s_sem, r_sem):
            self.buf, self.s_sem, self.r_sem = buf, s_sem, r_sem

        def put(self, p, kind, to):
            i = POS[p]
            b = at_pos(p, core)
            slot = {"ring": i, "sib": 16 + i, "x": 32}[kind]
            send(self.buf.at[b], self.buf.at[b], self.s_sem.at[slot], self.r_sem.at[self.target(p, kind)], dev(to))

        def target(self, p, kind):
            if kind == "sib":
                return 16 + POS[p]
            if kind == "x":
                return POS[(0, 1)]
            return None

        def ring(self, p, sign):
            q = (p[0] + sign, p[1])
            b = at_pos(p, core)
            send(
                self.buf.at[b], self.buf.at[b], self.s_sem.at[POS[q]], self.r_sem.at[POS[q]],
                dev(yup if sign < 0 else ydn),
            )

        def begin(self):
            p = (0, 0)
            self.ring(p, -1)
            self.ring(p, 1)
            self.put(p, "x", xnb)
            self.put(p, "sib", sib)

        def arrived(self, p):
            b = at_pos(p, core)
            wait_recv(self.buf.at[b], self.s_sem.at[0], self.r_sem.at[POS[p]])
            if p[0] == 0:
                self.ring(p, -1)
                self.ring(p, 1)
            else:
                sign = -1 if p[0] < 0 else 1
                if abs(p[0]) < last_of(sign, p[1]):
                    self.ring(p, sign)
            self.put(p, "sib", sib)

        def step(self, d):
            for p in POSITIONS:
                if abs(p[0]) == d and p != (0, 0):
                    self.arrived(p)

        def settle(self, d):
            for p in POSITIONS:
                if abs(p[0]) == d:
                    wait_recv(self.buf.at[at_pos(p, 1 - core)], self.s_sem.at[0], self.r_sem.at[16 + POS[p]])

    text_all = Gather(txt, txt_send, txt_recv)
    text_all.begin()
    send(p_send, p_recv, kv_send.at[0], kv_recv.at[0], dev(sib))
    text_all.step(0)

    wait_recv(p_recv, kv_send.at[0], kv_recv.at[0])
    csum[...] = part[pl.ds(pl.multiple_of(core * SLOTS, SLOTS), SLOTS), :] + p_recv[...].astype(F32)

    def head_sum(h):
        at = pl.multiple_of(h * HEAD_DIM, HEAD_DIM)
        return jnp.concatenate(
            [csum[:, pl.ds(at, HEAD_DIM)], csum[:, pl.ds(at + KV_HEADS * HEAD_DIM, HEAD_DIM)]], axis=1
        )

    def kv_up(k):
        val = head_sum((y + 4 - k) % Y)
        if k > 0:
            wait_recv(up_r.at[k - 1], kv_send.at[0], kv_recv.at[k])
            val = val + up_r[k - 1].astype(F32)
        up_s[k] = val.astype(BF16)
        send(up_s.at[k], up_r.at[k], kv_send.at[1 + k], kv_recv.at[1 + k], dev(yup))

    def kv_dn(k):
        val = head_sum((y + Y - 3 + k) % Y)
        if k > 0:
            wait_recv(dn_r.at[k - 1], kv_send.at[0], kv_recv.at[4 + k])
            val = val + dn_r[k - 1].astype(F32)
        dn_s[k] = val.astype(BF16)
        send(dn_s.at[k], dn_r.at[k], kv_send.at[5 + k], kv_recv.at[5 + k], dev(ydn))

    def project(y_list):
        rows = jnp.concatenate(
            [txt[pl.ds(yy * LANES, LANES)].astype(F32).reshape(LANES * 8, D) for yy in y_list], axis=0
        ).astype(BF16)
        res = jnp.dot(rows, wq[...], preferred_element_type=F32)
        for i, yy in enumerate(y_list):
            raw_q[pl.ds(pl.multiple_of(yy * 32, 32), 32), :] = res[i * 32 : i * 32 + 32]

    kv_up(0)
    kv_dn(0)
    text_all.step(1)
    kv_up(1)
    kv_dn(1)
    load_q.wait()
    text_all.settle(0)
    text_all.step(2)
    kv_up(2)
    kv_dn(2)
    text_all.settle(1)
    project([(y + Y - 1) % Y, (y + 1) % Y])
    text_all.step(3)
    kv_up(3)
    text_all.settle(2)
    project([(y + Y - 2) % Y, (y + 2) % Y])
    wait_recv(dn_r.at[2], kv_send.at[0], kv_recv.at[7])
    wait_recv(up_r.at[3], kv_send.at[0], kv_recv.at[4])
    x_s[...] = head_sum(y) + up_r[3].astype(F32) + dn_r[2].astype(F32)
    send(x_s, x_r, kv_send.at[8], kv_recv.at[8], dev(xnb))
    text_all.step(4)
    text_all.settle(3)
    project([(y + Y - 3) % Y, (y + 3) % Y])
    wait_recv(x_r, kv_send.at[0], kv_recv.at[8])
    kv[core] = x_s[...] + x_r[...]
    send(kv.at[core], kv.at[core], kv_send.at[9], kv_recv.at[9], dev(sib))
    text_all.settle(4)
    project([y, (y + 4) % Y])
    wait_recv(kv.at[1 - core], kv_send.at[0], kv_recv.at[9])

    rq = raw_q[...]
    q_all = (rq * lax.rsqrt(jnp.mean(rq * rq, axis=-1, keepdims=True) + EPS) * qg_ref[...].astype(F32)).astype(BF16)
    key_gain = kg_ref[...].astype(F32)
    slot_id = lax.broadcasted_iota(jnp.int32, (SLOTS, TXT_TOK), 0)
    row_id = lax.broadcasted_iota(jnp.int32, (TXT_TOK, HEAD_DIM), 0)
    pieces = []
    for b in range(MB):
        q = q_all[b * TXT_TOK : (b + 1) * TXT_TOK]
        key_raw = kv[b][:, :HEAD_DIM]
        values = kv[b][:, HEAD_DIM:].astype(BF16)
        inverse = lax.rsqrt(jnp.mean(key_raw * key_raw, axis=-1, keepdims=True) + EPS)
        key_hat = key_raw * inverse
        keys = (key_hat * key_gain).astype(BF16)
        row_live = (row_id >= is_ref[b]).astype(F32)
        scores = dotf(keys, q, ((1,), (1,))) * SCALE
        expo = jnp.where(slot_id < tc_ref[b] * TILE_LEN, jnp.exp(scores), 0.0)
        probs = expo / jnp.sum(expo, axis=0, keepdims=True)
        weights = probs.astype(BF16)
        att = dotf(weights, values, ((0,), (0,))) * row_live
        att_ref[pl.ds(b * TXT_TOK, TXT_TOK), :] = att.astype(BF16)
        upstream = (go_ref[pl.ds(b * TXT_TOK, TXT_TOK), :].astype(F32) * row_live).astype(BF16)
        d_weights = dotf(values, upstream, ((1,), (1,)))
        d_scores = (
            probs * (d_weights - jnp.sum(probs * d_weights, axis=0, keepdims=True)) * SCALE
        ).astype(BF16)
        d_keys = jnp.dot(d_scores, q, preferred_element_type=F32)
        d_values = jnp.dot(weights, upstream, preferred_element_type=F32)
        scaled = d_keys * key_gain
        d_raw = inverse * (scaled - key_hat * jnp.mean(key_hat * scaled, axis=-1, keepdims=True))
        pieces.append(jnp.concatenate([d_raw.astype(BF16), d_values.astype(BF16)], axis=1))
    for b in range(MB):
        for half in range(2):
            dq_s[b * 2 + half] = pieces[b][half * QUARTER : (half + 1) * QUARTER]

    for i, (t, k) in enumerate(((xnb, lane + 2 - 4 * xl), (diag, 3 - lane), (sib, lane + 1 - 2 * core))):
        send(dq_s.at[k], dq_r.at[lane], q_send.at[i], q_recv.at[i], dev(t))
    dq_r[lane] = dq_s[lane]
    for i, k in enumerate((lane + 2 - 4 * xl, 3 - lane, lane + 1 - 2 * core)):
        wait_recv(dq_r.at[k], q_send.at[0], q_recv.at[i])
    gath[me] = (
        dq_r[0].astype(F32) + dq_r[1].astype(F32) + dq_r[2].astype(F32) + dq_r[3].astype(F32)
    ).astype(BF16)

    def back(h):
        at = pl.multiple_of(h * HEAD_DIM, HEAD_DIM)
        d_kv = gath[pl.ds(h * LANES, LANES)].reshape(IMG, 2 * HEAD_DIM)
        return dotf(d_kv[:, :HEAD_DIM], wkv[:, pl.ds(at, HEAD_DIM)], ((1,), (1,))) + dotf(
            d_kv[:, HEAD_DIM:], wkv[:, pl.ds(at + KV_HEADS * HEAD_DIM, HEAD_DIM)], ((1,), (1,))
        )

    grad_all = Gather(gath, gat_send, gat_recv)
    grad_all.begin()
    for d in range(0, 5):
        grad_all.step(d)
        if d > 0:
            grad_all.settle(d - 1)
            if d == 1:
                grad[...] = back(y)
            else:
                grad[...] += back((y + Y - (d - 1)) % Y) + back((y + d - 1) % Y)
    grad_all.settle(4)
    total = grad[...] + back((y + 4) % Y)
    grad[...] = total
    sec_s[...] = total.reshape(N_SECTION, CHUNK, COLS).astype(BF16)

    for k in range(1, N_SECTION):
        to = (sec + k) % N_SECTION
        send(
            sec_s.at[to], sec_r.at[sec], s_send.at[k], s_recv.at[k], {"section": to, "tensor": me}
        )
    sec_r[sec] = jnp.zeros((CHUNK, COLS), BF16)
    for k in range(1, N_SECTION):
        wait_recv(sec_r.at[(sec + N_SECTION - k) % N_SECTION], s_send.at[0], s_recv.at[k])
    fg_ref[...] = grad[pl.ds(pl.multiple_of(sec * CHUNK, CHUNK), CHUNK), :] + jnp.sum(
        sec_r[...].astype(F32), axis=0
    )
    for copy in started:
        copy.wait_send()


def shards(
    text, features, in_gain, w_query, q_gain, w_key_value, k_gain, tile_count, image_start, grad_out
):
    vmem = pl.BlockSpec(memory_space=pltpu.VMEM)
    anyw = pl.BlockSpec(memory_space=pl.ANY)
    smem = pl.BlockSpec(memory_space=pltpu.SMEM)
    dma = pltpu.SemaphoreType.DMA
    attended, feature_grad = pl.pallas_call(
        kernel,
        name="cross",
        out_shape=(
            jax.ShapeDtypeStruct((MB * TXT_TOK, HEAD_DIM), BF16),
            jax.ShapeDtypeStruct((CHUNK, COLS), F32),
        ),
        in_specs=[vmem, vmem, vmem, anyw, vmem, anyw, vmem, smem, smem, vmem],
        out_specs=(vmem, vmem),
        scratch_shapes=[
            pltpu.VMEM((D, HEAD_DIM), BF16),
            pltpu.VMEM((COLS, 2 * KV_HEADS * HEAD_DIM), BF16),
            pltpu.VMEM((N_TENSOR, 8, D), BF16),
            pltpu.VMEM((MB * TXT_TOK, HEAD_DIM), F32),
            pltpu.VMEM((IMG, 2 * KV_HEADS * HEAD_DIM), F32),
            pltpu.VMEM((SLOTS, 2 * KV_HEADS * HEAD_DIM), BF16),
            pltpu.VMEM((SLOTS, 2 * KV_HEADS * HEAD_DIM), BF16),
            pltpu.VMEM((SLOTS, 2 * KV_HEADS * HEAD_DIM), F32),
            pltpu.VMEM((4, SLOTS, 2 * HEAD_DIM), BF16),
            pltpu.VMEM((4, SLOTS, 2 * HEAD_DIM), BF16),
            pltpu.VMEM((3, SLOTS, 2 * HEAD_DIM), BF16),
            pltpu.VMEM((3, SLOTS, 2 * HEAD_DIM), BF16),
            pltpu.VMEM((SLOTS, 2 * HEAD_DIM), F32),
            pltpu.VMEM((SLOTS, 2 * HEAD_DIM), F32),
            pltpu.VMEM((MB, SLOTS, 2 * HEAD_DIM), F32),
            pltpu.VMEM((LANES, QUARTER, 2 * HEAD_DIM), BF16),
            pltpu.VMEM((LANES, QUARTER, 2 * HEAD_DIM), BF16),
            pltpu.VMEM((N_TENSOR, QUARTER, 2 * HEAD_DIM), BF16),
            pltpu.VMEM((IMG, COLS), F32),
            pltpu.VMEM((N_SECTION, CHUNK, COLS), BF16),
            pltpu.VMEM((N_SECTION, CHUNK, COLS), BF16),
            dma((2,)),
            dma((33,)),
            dma((32,)),
            dma((33,)),
            dma((32,)),
            dma((10,)),
            dma((10,)),
            dma((3,)),
            dma((3,)),
            dma((N_SECTION,)),
            dma((N_SECTION,)),
        ],
        compiler_params=pltpu.CompilerParams(
            collective_id=0, has_side_effects=True, vmem_limit_bytes=48 * 1024 * 1024
        ),
    )(
        text[0], features, in_gain, w_query[0], q_gain, w_key_value[0], k_gain,
        tile_count, image_start, grad_out[0],
    )
    return (attended[None], feature_grad)


def solution(mesh):
    return jax.shard_map(
        shards,
        mesh=mesh,
        in_specs=(
            P("section", "tensor", None),
            P(None, "tensor"),
            P("section", None),
            P("section", None, "tensor"),
            P("section", None),
            P("section", "tensor", None),
            P("section", None),
            P(),
            P(),
            P("section", None, "tensor"),
        ),
        out_specs=(P("section", None, "tensor"), P("section", "tensor")),
        check_vma=False,
    )
```

time: 809 us -> 93.5 us (0.12)
  waiting for transfers between devices: 758 us -> 0 us
  Pallas kernels: 0 us -> 82.4 us
  between operations: 14 us -> 0.66 us
  other arithmetic: 11.7 us -> 0 us
  matrix products: 8.75 us -> 0 us
    reduce_scatter x1 -> x0, waiting for transfers between devices: 364 us -> none  [shards(): lax.psum_scatter(lax.dot_general(d_kv, weight_kv, (((1,), (1,)), ((), ())...]
    psum x1 -> x0, waiting for transfers between devices: 248 us -> none  [shards(): kv_full = lax.psum(partial_value, 'tensor')]
    all_gather x2 -> x0, waiting for transfers between devices: 145 us -> none  [the longest x1 73.8 us: shards(): piece = lax.all_gather(text[0], 'tensor', axis=0, tiled=True)]
    pallas_call x0 -> x1, Pallas kernels: none -> 82.4 us  [shards(): pl.pallas_call(kernel, name='cross', out_shape=(jax.ShapeDtypeStruct((MB...]
    reduce_sum x3 -> x0, other arithmetic: 10.7 us -> none  [the longest x1 6.4 us: shards(): gathered.reshape(KV_HEADS, per_kv, total_rows, 2, HEAD_DIM)]
    unnamed x16 -> x22, local copies, waits for them, and re-layouts: 0.21 us -> 10 us
    dot_general x8 -> x0, matrix products: 8.75 us -> none  [the longest x1 2.97 us: shards(): jnp.dot(features, weight_kv, preferred_element_type=jnp.float32)]
  transfers between devices with their start and end apart: 4 -> 0, of which waited for: 4 -> 0; matrix products, arithmetic and copies ran while one was open for 0% -> 0% of each run, Pallas kernels for 0% -> 0%
where the time goes in v1:
time: 93.5 us; the launch traced here: 93.1 us
  Pallas kernels  82.4 us (88%)
  local copies, waits for them, and re-layouts  10 us (11%)
    pallas_call x1, Pallas kernels, shards(): pl.pallas_call(kernel, name='cross', out_shape=(jax.ShapeDtypeStruct((MB...  82.4 us
    unnamed x22, local copies, waits for them, and re-layouts  10 us

profile of v1, /device:TPU:1, one launch (start us, length us, event | category | flops | bytes accessed | tf_op | source)
XLA Modules:
  0.0 93.1 jit_solution(15874048179082241164)
XLA Ops:
  0.6 0.0 copy-start
  0.6 1.6 %copy-done = bf16[1,8192,128]{2,1,0:T(8,128)(2,1)S(1)} copy-done((bf16[1,8192,128]{2,1,0:T(8,128)(2,1)S(1)}, bf16[1,8192,128]{2,1,0:T(8,128)(2,1)}, u32[]{:S(2)}) %copy-start) | copy-done | bytes 2097176
  2.2 0.0 copy-start.1
  2.2 1.2 %copy-done.1 = bf16[1,256,2048]{2,1,0:T(8,128)(2,1)S(1)} copy-done((bf16[1,256,2048]{2,1,0:T(8,128)(2,1)S(1)}, bf16[1,256,2048]{2,1,0:T(8,128)(2,1)}, u32[]{:S(2)}) %copy-start.1) | copy-done | bytes 1048600
  3.5 0.0 copy-start.2
  3.5 0.9 copy-done.2
  4.4 0.0 copy-start.3
  4.4 0.9 copy-done.3
  5.2 0.0 copy-start.4
  5.3 0.8 copy-done.4
  6.1 0.0 copy-start.5
  6.1 0.8 copy-done.5
  6.8 0.0 copy-start.6
  6.8 0.7 copy-done.6
  7.5 0.0 copy-start.7
  7.5 0.7 copy-done.7
  8.2 0.0 copy-start.8
  8.2 0.7 copy-done.8
  8.8 0.0 copy-start.9
  8.8 0.7 copy-done.9
  9.5 82.4 %cross.1 = (bf16[256,128]{1,0:T(8,128)(2,1)S(1)}, f32[8,256]{1,0:T(8,128)S(1)}) custom-call(bf16[8,8192]{1,0:T(8,128)(2,1)S(1)} %bitcast.7, bf16[192,256]{1,0:T(8,128)(2,1)S(1)} %copy-done.3, bf16[1,8192]{1,0:T(2,128)(2,1)S(1)} %copy-done.5, bf16[8192,128]{1,0:T(8,128)(2,1)S(1)} %bitcast.5, bf16[1,128]{1,0:T(2,128)(2,1)S(1)} %copy-done.6, ...), custom_call_target="tpu_custom_call" | custom-call | tf_op jit(solution)/shard_map/cross/pallas_call | solution.py:328
  91.9 0.6 copy.14
  92.5 0.6 copy.15
Async XLA Ops:
  0.6 1.6 %copy-start = (bf16[1,8192,128]{2,1,0:T(8,128)(2,1)S(1)}, bf16[1,8192,128]{2,1,0:T(8,128)(2,1)}, u32[]{:S(2)}) copy-start(bf16[1,8192,128]{2,1,0:T(8,128)(2,1)} %param.13) | copy-start | bytes 6291460
  2.2 1.2 %copy-start.1 = (bf16[1,256,2048]{2,1,0:T(8,128)(2,1)S(1)}, bf16[1,256,2048]{2,1,0:T(8,128)(2,1)}, u32[]{:S(2)}) copy-start(bf16[1,256,2048]{2,1,0:T(8,128)(2,1)} %param.15) | copy-start | bytes 3145732
  3.5 0.9 copy-start.2
  4.4 0.9 copy-start.3
  5.2 0.8 copy-start.4
  6.1 0.8 copy-start.5
  6.8 0.7 copy-start.6
  7.5 0.7 copy-start.7
  8.2 0.7 copy-start.8
  8.8 0.7 copy-start.9

commit v2 on v1

--- a/solution.py
+++ b/solution.py
@@ -24,6 +24,7 @@
 COLS = 256
 QUARTER = IMG // LANES
 CHUNK = IMG // N_SECTION
+CROSS = 6144
 SCALE = HEAD_DIM ** (-0.5)
 MESH = pl.DeviceIdType.MESH
 F32 = jnp.float32
@@ -39,18 +40,15 @@
 POS = {p: i for i, p in enumerate(POSITIONS)}
 
 
-def last_of(sign, other):
-    return 4 if (sign < 0) == (other == 0) else 3
-
-
 def dotf(a, b, dims):
     return lax.dot_general(a, b, (dims, ((), ())), preferred_element_type=F32)
 
 
 def kernel(
-    text_ref, feat_ref, ing_ref, wq_hbm, qg_ref, wkv_hbm, kg_ref, tc_ref, is_ref, go_ref,
-    att_ref, fg_ref,
-    wq, wkv, txt, raw_q, part, p_send, p_recv, csum, up_s, up_r, dn_s, dn_r,
+    text_hbm, feat_hbm, ing_hbm, wq_hbm, qg_hbm, wkv_hbm, kg_hbm, tc_hbm, is_hbm, go_hbm,
+    att_hbm, fg_hbm,
+    text_ref, feat_ref, ing_ref, qg_ref, kg_ref, tc_ref, is_ref, go_ref, att_ref, fg_ref,
+    wq, wkv, txt, raw_q, part, p_recv, csum, up_s, up_r, dn_s, dn_r,
     x_s, x_r, kv, dq_s, dq_r, gath, grad, sec_s, sec_r,
     w_sem, txt_send, txt_recv, gat_send, gat_recv, kv_send, kv_recv, q_send, q_recv, s_send, s_recv,
 ):
@@ -87,28 +85,38 @@
             src_ref=dst, dst_ref=dst, send_sem=s_sem, recv_sem=r_sem, device_id=dev(sib), device_id_type=MESH
         ).wait_recv()
 
+    loads = [
+        pltpu.make_async_copy(src, dst, w_sem.at[i])
+        for i, (src, dst) in enumerate(
+            (
+                (text_hbm, text_ref), (ing_hbm, ing_ref), (feat_hbm, feat_ref), (wkv_hbm, wkv), (wq_hbm, wq),
+                (go_hbm, go_ref), (qg_hbm, qg_ref), (kg_hbm, kg_ref), (tc_hbm, tc_ref), (is_hbm, is_ref),
+            )
+        )
+    ]
+    for load in loads:
+        load.start()
+
+    near = [yup, ydn, xnb, sib, diag, tid((y + 4) % Y, 1 - xl, core)]
+    near += [tid((y + d) % Y, xl, core) for d in (2, 3, 4, 5, 6)]
     barrier = pltpu.get_barrier_semaphore()
     for k in range(1, N_SECTION):
         pl.semaphore_signal(
             barrier, inc=1, device_id={"section": (sec + k) % N_SECTION, "tensor": me}, device_id_type=MESH
         )
-    for t in (yup, ydn, xnb, sib, diag):
+    for t in near:
         pl.semaphore_signal(barrier, inc=1, device_id=dev(t), device_id_type=MESH)
 
-    load_kv = pltpu.make_async_copy(wkv_hbm, wkv, w_sem.at[0])
-    load_q = pltpu.make_async_copy(wq_hbm, wq, w_sem.at[1])
-    load_kv.start()
-    load_q.start()
-
+    loads[0].wait()
+    loads[1].wait()
     own = text_ref[...].astype(F32)
     inv = lax.rsqrt(jnp.mean(own * own, axis=-1, keepdims=True) + EPS)
     txt[me] = (own * inv * ing_ref[...].astype(F32)).astype(BF16)
 
-    load_kv.wait()
-    part[...] = jnp.dot(feat_ref[...], wkv[...], preferred_element_type=F32)
-    p_send[...] = part[pl.ds(pl.multiple_of((1 - core) * SLOTS, SLOTS), SLOTS), :].astype(BF16)
-
-    pl.semaphore_wait(barrier, N_SECTION - 1 + 5)
+    def part_at(c_at):
+        return part.at[pl.ds(pl.multiple_of(c_at * SLOTS, SLOTS), SLOTS)]
+
+    pl.semaphore_wait(barrier, N_SECTION - 1 + len(near))
 
     def block(y_at, other, c_at):
         return tid(y_at, xl + other - 2 * xl * other, c_at)
@@ -116,67 +124,84 @@
     def at_pos(p, c_at):
         return block((y + p[0] + Y) % Y, p[1], c_at)
 
-    class Gather:
-        def __init__(self, buf, s_sem, r_sem):
-            self.buf, self.s_sem, self.r_sem = buf, s_sem, r_sem
-
-        def put(self, p, kind, to):
-            i = POS[p]
-            b = at_pos(p, core)
-            slot = {"ring": i, "sib": 16 + i, "x": 32}[kind]
-            send(self.buf.at[b], self.buf.at[b], self.s_sem.at[slot], self.r_sem.at[self.target(p, kind)], dev(to))
-
-        def target(self, p, kind):
-            if kind == "sib":
-                return 16 + POS[p]
-            if kind == "x":
-                return POS[(0, 1)]
-            return None
-
-        def ring(self, p, sign):
-            q = (p[0] + sign, p[1])
-            b = at_pos(p, core)
-            send(
-                self.buf.at[b], self.buf.at[b], self.s_sem.at[POS[q]], self.r_sem.at[POS[q]],
-                dev(yup if sign < 0 else ydn),
-            )
-
-        def begin(self):
-            p = (0, 0)
-            self.ring(p, -1)
-            self.ring(p, 1)
-            self.put(p, "x", xnb)
-            self.put(p, "sib", sib)
-
-        def arrived(self, p):
-            b = at_pos(p, core)
-            wait_recv(self.buf.at[b], self.s_sem.at[0], self.r_sem.at[POS[p]])
-            if p[0] == 0:
-                self.ring(p, -1)
-                self.ring(p, 1)
-            else:
-                sign = -1 if p[0] < 0 else 1
-                if abs(p[0]) < last_of(sign, p[1]):
-                    self.ring(p, sign)
-            self.put(p, "sib", sib)
-
-        def step(self, d):
-            for p in POSITIONS:
-                if abs(p[0]) == d and p != (0, 0):
-                    self.arrived(p)
-
-        def settle(self, d):
-            for p in POSITIONS:
-                if abs(p[0]) == d:
-                    wait_recv(self.buf.at[at_pos(p, 1 - core)], self.s_sem.at[0], self.r_sem.at[16 + POS[p]])
-
-    text_all = Gather(txt, txt_send, txt_recv)
-    text_all.begin()
-    send(p_send, p_recv, kv_send.at[0], kv_recv.at[0], dev(sib))
-    text_all.step(0)
+    parts = (pl.ds(0, CROSS), pl.ds(CROSS, D - CROSS))
+
+    def name(d, other):
+        return ((-4, 0), (4, 1))[other] if abs(d) == 4 else (d, other)
+
+    def text_ref_at(p, part, c_at):
+        return txt.at[at_pos(p, c_at), :, parts[part]]
+
+    def text_send(p, part, slot, r_slot, to):
+        ref = text_ref_at(p, part, core)
+        send(ref, ref, txt_send.at[slot], txt_recv.at[r_slot], dev(to))
+
+    def text_ring(d, other, part, sign):
+        far = d + sign
+        if abs(far) > (4 if (sign < 0) == (part == 0) else 3):
+            return
+        slot = POS[name(far, other)] * 2 + part
+        text_send(name(d, other), part, slot, slot, yup if sign < 0 else ydn)
+
+    def text_cross(p, part):
+        slot = POS[name(p[0], 1)] * 2 + part
+        text_send(p, part, 64 + POS[p] * 2 + part, slot, xnb)
+
+    def text_sib(p, part):
+        slot = 32 + POS[p] * 2 + part
+        text_send(p, part, slot, slot, sib)
+
+    def text_wait(p, part):
+        wait_recv(text_ref_at(p, part, core), txt_send.at[0], txt_recv.at[POS[p] * 2 + part])
+
+    def text_begin():
+        text_cross((0, 0), 1)
+        for part in range(2):
+            text_ring(0, 0, part, -1)
+            text_ring(0, 0, part, 1)
+        text_cross((0, 0), 0)
+        for part in range(2):
+            text_sib((0, 0), part)
+
+    def text_crossed(d):
+        for p in sorted({name(d, 1), name(-d, 1)}):
+            text_wait(p, 0)
+            text_sib(p, 0)
+
+    def text_step(d):
+        for other, part in ((0, 0), (0, 1), (1, 1)):
+            for sign in (-1, 1):
+                if d > (4 if (sign < 0) == (part == 0) else 3):
+                    continue
+                p = name(sign * d, other)
+                text_wait(p, part)
+                text_ring(sign * d, other, part, sign)
+                if part == 0:
+                    text_cross(p, 0)
+                text_sib(p, part)
+        text_crossed(d - 1)
+
+    def text_settle(d):
+        for p in POSITIONS:
+            if abs(p[0]) == d:
+                for part in range(2):
+                    wait_recv(
+                        text_ref_at(p, part, 1 - core), txt_send.at[0], txt_recv.at[32 + POS[p] * 2 + part]
+                    )
+
+    text_begin()
+
+    loads[2].wait()
+    loads[3].wait()
+    part[...] = jnp.dot(feat_ref[...], wkv[...], preferred_element_type=F32)
+    send(part_at(1 - core), p_recv, kv_send.at[0], kv_recv.at[0], dev(sib))
+    text_wait((0, 1), 1)
+    text_ring(0, 1, 1, -1)
+    text_ring(0, 1, 1, 1)
+    text_sib((0, 1), 1)
 
     wait_recv(p_recv, kv_send.at[0], kv_recv.at[0])
-    csum[...] = part[pl.ds(pl.multiple_of(core * SLOTS, SLOTS), SLOTS), :] + p_recv[...].astype(F32)
+    csum[...] = part_at(core)[...] + p_recv[...]
 
     def head_sum(h):
         at = pl.multiple_of(h * HEAD_DIM, HEAD_DIM)
@@ -188,16 +213,16 @@
         val = head_sum((y + 4 - k) % Y)
         if k > 0:
             wait_recv(up_r.at[k - 1], kv_send.at[0], kv_recv.at[k])
-            val = val + up_r[k - 1].astype(F32)
-        up_s[k] = val.astype(BF16)
+            val = val + up_r[k - 1]
+        up_s[k] = val
         send(up_s.at[k], up_r.at[k], kv_send.at[1 + k], kv_recv.at[1 + k], dev(yup))
 
     def kv_dn(k):
         val = head_sum((y + Y - 3 + k) % Y)
         if k > 0:
             wait_recv(dn_r.at[k - 1], kv_send.at[0], kv_recv.at[4 + k])
-            val = val + dn_r[k - 1].astype(F32)
-        dn_s[k] = val.astype(BF16)
+            val = val + dn_r[k - 1]
+        dn_s[k] = val
         send(dn_s.at[k], dn_r.at[k], kv_send.at[5 + k], kv_recv.at[5 + k], dev(ydn))
 
     def project(y_list):
@@ -210,31 +235,33 @@
 
     kv_up(0)
     kv_dn(0)
-    text_all.step(1)
+    text_step(1)
     kv_up(1)
     kv_dn(1)
-    load_q.wait()
-    text_all.settle(0)
-    text_all.step(2)
+    for load in loads[4:]:
+        load.wait()
+    text_step(2)
     kv_up(2)
     kv_dn(2)
-    text_all.settle(1)
+    text_settle(0)
+    text_settle(1)
     project([(y + Y - 1) % Y, (y + 1) % Y])
-    text_all.step(3)
+    text_step(3)
     kv_up(3)
-    text_all.settle(2)
+    text_settle(2)
     project([(y + Y - 2) % Y, (y + 2) % Y])
     wait_recv(dn_r.at[2], kv_send.at[0], kv_recv.at[7])
+    text_step(4)
     wait_recv(up_r.at[3], kv_send.at[0], kv_recv.at[4])
-    x_s[...] = head_sum(y) + up_r[3].astype(F32) + dn_r[2].astype(F32)
+    x_s[...] = head_sum(y) + up_r[3] + dn_r[2]
     send(x_s, x_r, kv_send.at[8], kv_recv.at[8], dev(xnb))
-    text_all.step(4)
-    text_all.settle(3)
+    text_settle(3)
     project([(y + Y - 3) % Y, (y + 3) % Y])
+    text_crossed(4)
     wait_recv(x_r, kv_send.at[0], kv_recv.at[8])
     kv[core] = x_s[...] + x_r[...]
     send(kv.at[core], kv.at[core], kv_send.at[9], kv_recv.at[9], dev(sib))
-    text_all.settle(4)
+    text_settle(4)
     project([y, (y + 4) % Y])
     wait_recv(kv.at[1 - core], kv_send.at[0], kv_recv.at[9])
 
@@ -281,6 +308,9 @@
         dq_r[0].astype(F32) + dq_r[1].astype(F32) + dq_r[2].astype(F32) + dq_r[3].astype(F32)
     ).astype(BF16)
 
+    store_att = pltpu.make_async_copy(att_ref, att_hbm, w_sem.at[10])
+    store_att.start()
+
     def back(h):
         at = pl.multiple_of(h * HEAD_DIM, HEAD_DIM)
         d_kv = gath[pl.ds(h * LANES, LANES)].reshape(IMG, 2 * HEAD_DIM)
@@ -288,22 +318,56 @@
             d_kv[:, HEAD_DIM:], wkv[:, pl.ds(at + KV_HEADS * HEAD_DIM, HEAD_DIM)], ((1,), (1,))
         )
 
-    grad_all = Gather(gath, gat_send, gat_recv)
-    grad_all.begin()
-    for d in range(0, 5):
-        grad_all.step(d)
-        if d > 0:
-            grad_all.settle(d - 1)
-            if d == 1:
-                grad[...] = back(y)
-            else:
-                grad[...] += back((y + Y - (d - 1)) % Y) + back((y + d - 1) % Y)
-    grad_all.settle(4)
-    total = grad[...] + back((y + 4) % Y)
+    def grad_send(p, slot, r_slot, to):
+        ref = gath.at[at_pos(p, core)]
+        send(ref, ref, gat_send.at[slot], gat_recv.at[r_slot], dev(to))
+
+    def grad_direct(d, other):
+        slot = POS[name(-d, other)]
+        grad_send((0, 0), slot, slot, tid((y + d + Y) % Y, xl + other - 2 * xl * other, core))
+
+    def grad_cross(p):
+        grad_send(p, 32 + POS[p], POS[name(p[0], 1)], xnb)
+
+    def grad_sib(p):
+        grad_send(p, 16 + POS[p], 16 + POS[p], sib)
+
+    def grad_wait(p):
+        wait_recv(gath.at[at_pos(p, core)], gat_send.at[0], gat_recv.at[POS[p]])
+
+    def grad_settle(d):
+        for p in POSITIONS:
+            if abs(p[0]) == d:
+                wait_recv(gath.at[at_pos(p, 1 - core)], gat_send.at[0], gat_recv.at[16 + POS[p]])
+
+    for d, other in ((1, 0), (-1, 0), (2, 0), (-2, 0), (3, 0), (-3, 0), (4, 1), (4, 0)):
+        grad_direct(d, other)
+    grad_cross((0, 0))
+    grad_sib((0, 0))
+    for d in (1, 2, 3):
+        for p in ((-d, 0), (d, 0)):
+            grad_wait(p)
+            grad_cross(p)
+            grad_sib(p)
+        for p in sorted({(1 - d, 1), (d - 1, 1)}):
+            grad_wait(p)
+            grad_sib(p)
+    for p in ((-4, 0), (4, 1), (-3, 1), (3, 1)):
+        grad_wait(p)
+        grad_sib(p)
+    grad_settle(0)
+    grad[...] = back(y)
+    for d in (1, 2):
+        grad_settle(d)
+        grad[...] += back((y + Y - d) % Y) + back((y + d) % Y)
+    grad_settle(4)
+    grad[...] += back((y + 4) % Y)
+    grad_settle(3)
+    total = grad[...] + back((y + Y - 3) % Y) + back((y + 3) % Y)
     grad[...] = total
     sec_s[...] = total.reshape(N_SECTION, CHUNK, COLS).astype(BF16)
 
-    for k in range(1, N_SECTION):
+    for k in sorted(range(1, N_SECTION), key=lambda k: -min(k, N_SECTION - k)):
         to = (sec + k) % N_SECTION
         send(
             sec_s.at[to], sec_r.at[sec], s_send.at[k], s_recv.at[k], {"section": to, "tensor": me}
@@ -314,16 +378,18 @@
     fg_ref[...] = grad[pl.ds(pl.multiple_of(sec * CHUNK, CHUNK), CHUNK), :] + jnp.sum(
         sec_r[...].astype(F32), axis=0
     )
+    store_fg = pltpu.make_async_copy(fg_ref, fg_hbm, w_sem.at[11])
+    store_fg.start()
     for copy in started:
         copy.wait_send()
+    store_att.wait()
+    store_fg.wait()
 
 
 def shards(
     text, features, in_gain, w_query, q_gain, w_key_value, k_gain, tile_count, image_start, grad_out
 ):
-    vmem = pl.BlockSpec(memory_space=pltpu.VMEM)
-    anyw = pl.BlockSpec(memory_space=pl.ANY)
-    smem = pl.BlockSpec(memory_space=pltpu.SMEM)
+    hbm = pl.BlockSpec(memory_space=pltpu.HBM)
     dma = pltpu.SemaphoreType.DMA
     attended, feature_grad = pl.pallas_call(
         kernel,
@@ -332,21 +398,30 @@
             jax.ShapeDtypeStruct((MB * TXT_TOK, HEAD_DIM), BF16),
             jax.ShapeDtypeStruct((CHUNK, COLS), F32),
         ),
-        in_specs=[vmem, vmem, vmem, anyw, vmem, anyw, vmem, smem, smem, vmem],
-        out_specs=(vmem, vmem),
+        in_specs=[hbm] * 10,
+        out_specs=(hbm, hbm),
         scratch_shapes=[
+            pltpu.VMEM((8, D), BF16),
+            pltpu.VMEM((IMG, COLS), BF16),
+            pltpu.VMEM((1, D), BF16),
+            pltpu.VMEM((1, HEAD_DIM), BF16),
+            pltpu.VMEM((1, HEAD_DIM), BF16),
+            pltpu.SMEM((MB,), jnp.int32),
+            pltpu.SMEM((MB,), jnp.int32),
+            pltpu.VMEM((MB * TXT_TOK, HEAD_DIM), BF16),
+            pltpu.VMEM((MB * TXT_TOK, HEAD_DIM), BF16),
+            pltpu.VMEM((CHUNK, COLS), F32),
             pltpu.VMEM((D, HEAD_DIM), BF16),
             pltpu.VMEM((COLS, 2 * KV_HEADS * HEAD_DIM), BF16),
             pltpu.VMEM((N_TENSOR, 8, D), BF16),
             pltpu.VMEM((MB * TXT_TOK, HEAD_DIM), F32),
             pltpu.VMEM((IMG, 2 * KV_HEADS * HEAD_DIM), F32),
-            pltpu.VMEM((SLOTS, 2 * KV_HEADS * HEAD_DIM), BF16),
-            pltpu.VMEM((SLOTS, 2 * KV_HEADS * HEAD_DIM), BF16),
             pltpu.VMEM((SLOTS, 2 * KV_HEADS * HEAD_DIM), F32),
-            pltpu.VMEM((4, SLOTS, 2 * HEAD_DIM), BF16),
-            pltpu.VMEM((4, SLOTS, 2 * HEAD_DIM), BF16),
-            pltpu.VMEM((3, SLOTS, 2 * HEAD_DIM), BF16),
-            pltpu.VMEM((3, SLOTS, 2 * HEAD_DIM), BF16),
+            pltpu.VMEM((SLOTS, 2 * KV_HEADS * HEAD_DIM), F32),
+            pltpu.VMEM((4, SLOTS, 2 * HEAD_DIM), F32),
+            pltpu.VMEM((4, SLOTS, 2 * HEAD_DIM), F32),
+            pltpu.VMEM((3, SLOTS, 2 * HEAD_DIM), F32),
+            pltpu.VMEM((3, SLOTS, 2 * HEAD_DIM), F32),
             pltpu.VMEM((SLOTS, 2 * HEAD_DIM), F32),
             pltpu.VMEM((SLOTS, 2 * HEAD_DIM), F32),
             pltpu.VMEM((MB, SLOTS, 2 * HEAD_DIM), F32),
@@ -356,10 +431,10 @@
             pltpu.VMEM((IMG, COLS), F32),
             pltpu.VMEM((N_SECTION, CHUNK, COLS), BF16),
             pltpu.VMEM((N_SECTION, CHUNK, COLS), BF16),
-            dma((2,)),
-            dma((33,)),
-            dma((32,)),
-            dma((33,)),
+            dma((12,)),
+            dma((96,)),
+            dma((64,)),
+            dma((48,)),
             dma((32,)),
             dma((10,)),
             dma((10,)),
@@ -369,7 +444,7 @@
             dma((N_SECTION,)),
         ],
         compiler_params=pltpu.CompilerParams(
-            collective_id=0, has_side_effects=True, vmem_limit_bytes=48 * 1024 * 1024
+            collective_id=0, has_side_effects=True, vmem_limit_bytes=60 * 1024 * 1024
         ),
     )(
         text[0], features, in_gain, w_query[0], q_gain, w_key_value[0], k_gain,

time: 93.5 us -> 80.4 us (0.86)
  local copies, waits for them, and re-layouts: 10 us -> 2.77 us
  Pallas kernels: 82.4 us -> 76.4 us
    unnamed x22 -> x2, local copies, waits for them, and re-layouts: 10 us -> 2.77 us
    pallas_call x1, Pallas kernels: 82.4 us -> 76.4 us  [shards(): pl.pallas_call(kernel, name='cross', out_shape=(jax.ShapeDtypeStruct((MB...]
where the time goes in v2:
time: 80.4 us; the launch traced here: 79.8 us
  Pallas kernels  76.4 us (95%)
  local copies, waits for them, and re-layouts  2.77 us (3%)
    pallas_call x1, Pallas kernels, shards(): pl.pallas_call(kernel, name='cross', out_shape=(jax.ShapeDtypeStruct((MB...  76.4 us
    unnamed x2, local copies, waits for them, and re-layouts  2.77 us

profile of v2, /device:TPU:1, one launch (start us, length us, event | category | flops | bytes accessed | tf_op | source)
XLA Modules:
  0.0 79.8 jit_solution(13853032118483486427)
XLA Ops:
  0.6 76.4 %cross.1 = (bf16[256,128]{1,0:T(8,128)(2,1)}, f32[8,256]{1,0:T(8,128)}) custom-call(bf16[8,8192]{1,0:T(8,128)(2,1)} %bitcast.7, bf16[192,256]{1,0:T(8,128)(2,1)} %feat_hbm.1, bf16[1,8192]{1,0:T(2,128)(2,1)} %ing_hbm.1, bf16[8192,128]{1,0:T(8,128)(2,1)} %bitcast.5, bf16[1,128]{1,0:T(2,128)(2,1)} %qg_hbm.1, bf16[256,2048]{1,0:T(8,128)(2,1)} %bitcast.6, ...), custom_call_target="tpu_custom_call" | custom-call | tf_op jit(solution)/shard_map/cross/pallas_call | solution.py:394
  77.1 1.5 %copy.14 = bf16[1,256,128]{2,1,0:T(8,128)(2,1)} copy(bf16[1,256,128]{2,1,0:T(8,128)(2,1)} %bitcast.9) | data formatting | bytes 131072
  78.6 1.3 %copy.15 = f32[8,256]{1,0:T(8,128)} copy(f32[8,256]{1,0:T(8,128)} %get-tuple-element.9) | data formatting | bytes 16384

commit v3 on v2

--- a/solution.py
+++ b/solution.py
@@ -24,6 +24,7 @@
 COLS = 256
 QUARTER = IMG // LANES
 CHUNK = IMG // N_SECTION
+HOPS = 6
 CROSS = 6144
 SCALE = HEAD_DIM ** (-0.5)
 MESH = pl.DeviceIdType.MESH
@@ -50,7 +51,7 @@
     text_ref, feat_ref, ing_ref, qg_ref, kg_ref, tc_ref, is_ref, go_ref, att_ref, fg_ref,
     wq, wkv, txt, raw_q, part, p_recv, csum, up_s, up_r, dn_s, dn_r,
     x_s, x_r, kv, dq_s, dq_r, gath, grad, sec_s, sec_r,
-    w_sem, txt_send, txt_recv, gat_send, gat_recv, kv_send, kv_recv, q_send, q_recv, s_send, s_recv,
+    w_sem, txt_send, txt_recv, gat_send, gat_recv, kv_send, kv_recv, q_send, q_recv, s_send, s_recv, hop,
 ):
     sec = lax.axis_index("section")
     me = lax.axis_index("tensor")
@@ -100,10 +101,9 @@
     near = [yup, ydn, xnb, sib, diag, tid((y + 4) % Y, 1 - xl, core)]
     near += [tid((y + d) % Y, xl, core) for d in (2, 3, 4, 5, 6)]
     barrier = pltpu.get_barrier_semaphore()
-    for k in range(1, N_SECTION):
-        pl.semaphore_signal(
-            barrier, inc=1, device_id={"section": (sec + k) % N_SECTION, "tensor": me}, device_id_type=MESH
-        )
+    sec_up, sec_dn = (sec + 2) % N_SECTION, (sec + N_SECTION - 2) % N_SECTION
+    for to in (sec_up, sec_dn, sec + 1 - 2 * (sec % 2)):
+        pl.semaphore_signal(barrier, inc=1, device_id={"section": to, "tensor": me}, device_id_type=MESH)
     for t in near:
         pl.semaphore_signal(barrier, inc=1, device_id=dev(t), device_id_type=MESH)
 
@@ -116,7 +116,18 @@
     def part_at(c_at):
         return part.at[pl.ds(pl.multiple_of(c_at * SLOTS, SLOTS), SLOTS)]
 
-    pl.semaphore_wait(barrier, N_SECTION - 1 + len(near))
+    pl.semaphore_wait(barrier, 3 + len(near))
+
+    def section_step(r):
+        if r > 0:
+            for way in range(2):
+                pl.semaphore_wait(hop.at[r - 1, way], 1)
+        if r < HOPS:
+            for way, to in enumerate((sec_up, sec_dn)):
+                pl.semaphore_signal(
+                    hop.at[r, way], inc=1, device_id={"section": to, "tensor": me}, device_id_type=MESH
+                )
+
 
     def block(y_at, other, c_at):
         return tid(y_at, xl + other - 2 * xl * other, c_at)
@@ -233,30 +244,36 @@
         for i, yy in enumerate(y_list):
             raw_q[pl.ds(pl.multiple_of(yy * 32, 32), 32), :] = res[i * 32 : i * 32 + 32]
 
+    section_step(0)
     kv_up(0)
     kv_dn(0)
+    section_step(1)
     text_step(1)
     kv_up(1)
     kv_dn(1)
     for load in loads[4:]:
         load.wait()
+    section_step(2)
     text_step(2)
     kv_up(2)
     kv_dn(2)
     text_settle(0)
     text_settle(1)
     project([(y + Y - 1) % Y, (y + 1) % Y])
+    section_step(3)
     text_step(3)
     kv_up(3)
     text_settle(2)
     project([(y + Y - 2) % Y, (y + 2) % Y])
     wait_recv(dn_r.at[2], kv_send.at[0], kv_recv.at[7])
+    section_step(4)
     text_step(4)
     wait_recv(up_r.at[3], kv_send.at[0], kv_recv.at[4])
     x_s[...] = head_sum(y) + up_r[3] + dn_r[2]
     send(x_s, x_r, kv_send.at[8], kv_recv.at[8], dev(xnb))
     text_settle(3)
     project([(y + Y - 3) % Y, (y + 3) % Y])
+    section_step(5)
     text_crossed(4)
     wait_recv(x_r, kv_send.at[0], kv_recv.at[8])
     kv[core] = x_s[...] + x_r[...]
@@ -367,6 +384,7 @@
     grad[...] = total
     sec_s[...] = total.reshape(N_SECTION, CHUNK, COLS).astype(BF16)
 
+    section_step(6)
     for k in sorted(range(1, N_SECTION), key=lambda k: -min(k, N_SECTION - k)):
         to = (sec + k) % N_SECTION
         send(
@@ -442,6 +460,7 @@
             dma((3,)),
             dma((N_SECTION,)),
             dma((N_SECTION,)),
+            pltpu.SemaphoreType.REGULAR((HOPS, 2)),
         ],
         compiler_params=pltpu.CompilerParams(
             collective_id=0, has_side_effects=True, vmem_limit_bytes=60 * 1024 * 1024

time: 80.4 us -> 79 us (0.983)
  Pallas kernels: 76.4 us -> 75.4 us
    pallas_call x1, Pallas kernels: 76.4 us -> 75.4 us  [shards(): pl.pallas_call(kernel, name='cross', out_shape=(jax.ShapeDtypeStruct((MB...]
where the time goes in v3:
time: 79 us; the launch traced here: 78.8 us
  Pallas kernels  75.4 us (95%)
  local copies, waits for them, and re-layouts  2.77 us (4%)
    pallas_call x1, Pallas kernels, shards(): pl.pallas_call(kernel, name='cross', out_shape=(jax.ShapeDtypeStruct((MB...  75.4 us
    unnamed x2, local copies, waits for them, and re-layouts  2.77 us

profile of v3, /device:TPU:1, one launch (start us, length us, event | category | flops | bytes accessed | tf_op | source)
XLA Modules:
  0.0 78.8 jit_solution(7787060676875239663)
XLA Ops:
  0.6 75.4 %cross.1 = (bf16[256,128]{1,0:T(8,128)(2,1)}, f32[8,256]{1,0:T(8,128)}) custom-call(bf16[8,8192]{1,0:T(8,128)(2,1)} %bitcast.7, bf16[192,256]{1,0:T(8,128)(2,1)} %feat_hbm.1, bf16[1,8192]{1,0:T(2,128)(2,1)} %ing_hbm.1, bf16[8192,128]{1,0:T(8,128)(2,1)} %bitcast.5, bf16[1,128]{1,0:T(2,128)(2,1)} %qg_hbm.1, bf16[256,2048]{1,0:T(8,128)(2,1)} %bitcast.6, ...), custom_call_target="tpu_custom_call" | custom-call | tf_op jit(solution)/shard_map/cross/pallas_call | solution.py:412
  76.0 1.5 %copy.14 = bf16[1,256,128]{2,1,0:T(8,128)(2,1)} copy(bf16[1,256,128]{2,1,0:T(8,128)(2,1)} %bitcast.9) | data formatting | bytes 131072
  77.5 1.3 %copy.15 = f32[8,256]{1,0:T(8,128)} copy(f32[8,256]{1,0:T(8,128)} %get-tuple-element.9) | data formatting | bytes 16384
